TPU v7x, 128 devices: a whole 4x4x4 slice. The times are simulated.
128 devices in a mesh: occ: 4 (over x), vir: 32 (over y, z, core).
Axes of the slice: x: 4, y: 4, z: 4, core: 2. Of those that a mesh axis runs over, the one named last changes fastest.
Arguments:
- amplitudes: bfloat16 [256, 262144], P('occ', 'vir'), may hold values from -6 to 6
- cycle_integrals: bfloat16 [16, 64, 16, 64], P(None, None, 'occ'), may hold values from -0.1875 to 0.1875
- ladder_tiles: bfloat16 [2048, 4, 128, 128], P('vir'), may hold values from -0.25 to 0.25
- ladder_rows: int32 [2048, 4], P('vir'), may hold values from 0 to 2047, as said below
- ladder_count: int32 [2048], P('vir'), may hold values from 2 to 4
- row_gap: float32 [256], P('occ'), may hold values from 1 to 3
- column_energy: float32 [262144], P('vir'), may hold values from 0.5 to 8
Outputs:
- updated: bfloat16 [256, 262144], P('occ', 'vir')
Inputs may be any that keep to these rules, and one draw needn't show every extreme that they name: `ladder_rows`: each entry of column tile c's list names a virtual-pair tile within 2 tiles of c; entry 0 is max(c - 2, 0) and entry 1 is min(c + 2, 2047).
All inputs are finite; a program needn't handle non-finite values.
Results may differ from a plain program's by a relative error of at most 0.0019.
Values may be sent and summed in bfloat16 or wider, within the bound.
A program may use at most 192 MiB of HBM per device.

v0:
```python
import jax
import jax.numpy as jnp
from jax import lax
from jax.sharding import PartitionSpec as P

TILE = 128
NJ = 16
NA = 4096
NB_DEV = 2
KMAX = 4
HT = 2


def extended(block, sides, width):
    for axis, dim in sides:
        count = lax.axis_size(axis)
        forward = [(i, i + 1) for i in range(count - 1)]
        backward = [(target, source) for source, target in forward]
        low = lax.ppermute(
            lax.slice_in_dim(block, block.shape[dim] - width, None, axis=dim), axis, forward
        )
        high = lax.ppermute(lax.slice_in_dim(block, 0, width, axis=dim), axis, backward)
        block = jnp.concatenate([low, block, high], axis=dim)
    return block


def local(
    amplitudes, cycle_integrals, ladder_tiles, ladder_rows, ladder_count, row_gap, column_energy
):
    rows_dev = amplitudes.shape[0]
    cols_dev = amplitudes.shape[1]
    outer_occ = rows_dev // NJ
    four_dim = amplitudes.reshape(outer_occ, NJ, NB_DEV, NA)
    cycle_input = lax.all_to_all(four_dim, "vir", split_axis=3, concat_axis=2, tiled=True)
    tiles_dev = cols_dev // TILE
    padded = extended(amplitudes, (("vir", 1),), HT * TILE)
    own_tiles = lax.axis_index("vir") * tiles_dev + jnp.arange(tiles_dev, dtype=jnp.int32)
    relative = ladder_rows - own_tiles[:, None]
    live_mask = jnp.arange(KMAX, dtype=jnp.int32)[None, :] < ladder_count[:, None]
    ladder = jnp.zeros((rows_dev, tiles_dev, TILE), jnp.float32)
    for offset in range(2 * HT + 1):
        window = padded[:, offset * TILE : offset * TILE + cols_dev].reshape(
            rows_dev, tiles_dev, TILE
        )
        for entry in range(KMAX):
            selected = live_mask[:, entry] & (relative[:, entry] == offset - HT)
            masked = jnp.where(
                selected[:, None, None], ladder_tiles[:, entry], jnp.zeros((), jnp.bfloat16)
            )
            ladder = ladder + jnp.einsum(
                "rcp,cpq->rcq", window, masked, preferred_element_type=jnp.float32
            )
    ladder = ladder.reshape(rows_dev, cols_dev)
    all_rows = lax.all_gather(cycle_input, "occ", axis=0, tiled=True)
    cycle_part = jnp.einsum(
        "ijba,jbkc->ikca", all_rows, cycle_integrals, preferred_element_type=jnp.float32
    ).astype(jnp.bfloat16)
    cycle_pair = lax.all_to_all(
        lax.all_to_all(cycle_part, "occ", split_axis=0, concat_axis=1, tiled=True),
        "vir",
        split_axis=2,
        concat_axis=3,
        tiled=True,
    )
    cycle_flat = cycle_pair.reshape(rows_dev, cols_dev)
    denominator = row_gap[:, None] + column_energy[None, :]
    updated = (
        amplitudes.astype(jnp.float32) + (cycle_flat.astype(jnp.float32) + ladder) / denominator
    )
    return updated.astype(jnp.bfloat16)


def solution(mesh):
    in_specs = (
        P("occ", "vir"),
        P(None, None, "occ", None),
        P("vir", None, None, None),
        P("vir", None),
        P("vir"),
        P("occ"),
        P("vir"),
    )
    out_specs = P("occ", "vir")
    return jax.shard_map(local, mesh=mesh, in_specs=in_specs, out_specs=out_specs, check_vma=False)
```

profile of v0, /device:TPU:1, one launch (start us, length us, event | category | flops | bytes accessed | tf_op | source)
XLA Modules:
  0.0 195.1 jit_solution(11123908715003614297)
XLA Ops:
  6.5 0.8 fusion.152
  7.3 4.9 %collective-permute-start = (bf16[64,256]{1,0:T(8,128)(2,1)S(1)}, bf16[64,256]{1,0:T(8,128)(2,1)S(1)}, u32[]{:S(2)}, u32[]{:S(2)}) collective-permute-start(bf16[64,256]{1,0:T(8,128)(2,1)S(1)} %get-tuple-element.11), channel_id=1, source_target_pairs={{0,1},{1,2},{2,3},{3,4},{4,5},{5,6},{6,7},{7,8},{8,9},{9,10},{10,1... | collective-permute-start | bytes 98312 | tf_op jit(solution)/shard_map/ppermute | solution.py:19
  12.2 1.9 collective-permute-start.1
  14.2 1.8 reshape.294
  16.0 9.4 %copy.133 = bf16[4,16,2,4096]{1,0,2,3:T(4,128)(2,1)} copy(bf16[4,16,2,4096]{3,2,1,0:T(2,128)(2,1)S(1)} %reshape.294) | data formatting | bytes 2097152 | tf_op jit(solution)/shard_map/reshape | solution.py:33
  25.5 11.2 %reshape.306 = bf16[32,2,8192]{2,1,0:T(2,128)(2,1)} reshape(bf16[4096,2,4,16]{3,2,1,0:T(4,128)(2,1)} %bitcast.213) | data formatting | bytes 2097152
  36.7 8.4 %all-to-all-start = ((bf16[32,2,8192]{2,1,0:T(2,128)(2,1)}), bf16[32,2,8192]{2,1,0:T(2,128)(2,1)S(1)}, u32[]{:S(2)}, u32[]{:S(2)}) async-start(bf16[32,2,8192]{2,1,0:T(2,128)(2,1)} %reshape.306), calls=%async_computation | async-start | bytes 2097152 | tf_op jit(solution)/shard_map/all_to_all | solution.py:34
  45.1 0.0 all-gather.2.cloned.1.call-start
  45.2 0.0 copy-done.7
  45.2 0.0 copy-done.4
  45.3 0.0 copy-done
  45.3 3.7 %fusion.12 = f32[64,128,64]{1,2,0:T(8,128)} fusion(pred[64]{0:T(512)(128)(4,1)S(1)} %get-tuple-element.23, bf16[64,4,128,128]{3,2,1,0:T(8,128)(2,1)} %param.9, bf16[64,8192]{1,0:T(8,128)(2,1)S(1)} %copy-done), kind=kOutput, calls=%fused_computation.23 | convolution fusion | flops 135266304 | bytes 5242944 | tf_op jit(solution)/shard_map/rcp,cpq->rcq/dot_general | solution.py:50
  49.0 3.6 %fusion.17 = f32[64,128,64]{1,2,0:T(8,128)} fusion(pred[64]{0:T(512)(128)(4,1)S(1)} %get-tuple-element.15, bf16[64,4,128,128]{3,2,1,0:T(8,128)(2,1)} %param.9, bf16[64,8192]{1,0:T(8,128)(2,1)S(1)} %copy-done), kind=kOutput, calls=%fused_computation.33 | convolution fusion | flops 135266304 | bytes 5242944 | tf_op jit(solution)/shard_map/rcp,cpq->rcq/dot_general | solution.py:50
  52.7 3.7 %fusion.23 = f32[64,128,64]{1,2,0:T(8,128)} fusion(pred[64]{0:T(512)(128)(4,1)S(1)} %get-tuple-element.19, bf16[64,4,128,128]{3,2,1,0:T(8,128)(2,1)} %param.9, bf16[64,8192]{1,0:T(8,128)(2,1)S(1)} %copy-done), kind=kOutput, calls=%fused_computation.48 | convolution fusion | flops 135266304 | bytes 5242944 | tf_op jit(solution)/shard_map/rcp,cpq->rcq/dot_general | solution.py:50
  56.3 5.7 %all-to-all-done = bf16[32,2,8192]{2,1,0:T(2,128)(2,1)S(1)} async-done(((bf16[32,2,8192]{2,1,0:T(2,128)(2,1)}), bf16[32,2,8192]{2,1,0:T(2,128)(2,1)S(1)}, u32[]{:S(2)}, u32[]{:S(2)}) %all-to-all-start) | async-done | bytes 1048608 | tf_op jit(solution)/shard_map/all_to_all | solution.py:34
  62.0 7.6 %reshape.307 = bf16[4096,2,4,16]{3,2,1,0:T(4,128)(2,1)} reshape(bf16[32,2,8192]{2,1,0:T(2,128)(2,1)S(1)} %all-to-all-done) | data formatting | bytes 2097152
  69.6 12.8 %copy.134 = bf16[4,16,32,2,128]{4,3,2,1,0:T(2,128)(2,1)} copy(bf16[4,16,32,2,128]{1,0,3,4,2:T(4,128)(2,1)} %bitcast.214) | data formatting | bytes 2097152 | tf_op jit(solution)/shard_map/all_to_all | solution.py:34
  82.4 0.0 all-gather.2.cloned.1.call-update
  82.4 0.0 slice-start
  82.4 3.9 %fusion.7 = f32[64,128,64]{1,2,0:T(8,128)} fusion(pred[64]{0:T(512)(128)(4,1)S(1)} %get-tuple-element.27, bf16[64,4,128,128]{3,2,1,0:T(8,128)(2,1)} %param.9, bf16[64,8192]{1,0:T(8,128)(2,1)S(1)} %copy-done), kind=kOutput, calls=%fused_computation.13 | convolution fusion | flops 135266304 | bytes 5242944 | tf_op jit(solution)/shard_map/rcp,cpq->rcq/dot_general | solution.py:50
  86.3 0.0 collective-permute-done
  86.3 0.0 slice-start.1
  86.4 0.1 constant_dynamic-update-slice_fusion
  86.5 0.0 collective-permute-done.1
  86.5 0.4 slice_bitcast_fusion.1
  86.9 0.0 copy-start.1
  86.9 0.3 slice_bitcast_fusion.3
  87.2 0.0 copy-start.2
  87.2 0.0 slice-done
  87.2 2.2 %slice-done.1 = s8[4194304]{0:T(1024)(128)(4,1)S(1)} async-done(((s8[8388608]{0:T(1024)(128)(4,1)}), s8[4194304]{0:T(1024)(128)(4,1)S(1)}, s32[]{:S(2)}) %slice-start.1) | async-done | bytes 4194328
  89.4 2.1 %fusion.13 = f32[64,128,64]{1,2,0:T(8,128)} fusion(pred[64]{0:T(512)(128)(4,1)S(1)} %get-tuple-element.24, bf16[64,4,128,128]{3,2,1,0:T(8,128)(2,1)S(1)} %bitcast.220, bf16[8,64,8,128]{3,2,1,0:T(8,128)(2,1)S(1)} %get-tuple-element.7), kind=kOutput, calls=%fused_computation.24 | convolution fusion | flops 135266304 | bytes 5243392 | tf_op jit(solution)/shard_map/rcp,cpq->rcq/dot_general | solution.py:50
  91.5 2.1 %fusion.18 = f32[64,128,64]{1,2,0:T(8,128)} fusion(pred[64]{0:T(512)(128)(4,1)S(1)} %get-tuple-element.16, bf16[64,4,128,128]{3,2,1,0:T(8,128)(2,1)S(1)} %bitcast.220, bf16[8,64,8,128]{3,2,1,0:T(8,128)(2,1)S(1)} %get-tuple-element.7), kind=kOutput, calls=%fused_computation.34 | convolution fusion | flops 135266304 | bytes 5243392 | tf_op jit(solution)/shard_map/rcp,cpq->rcq/dot_general | solution.py:50
  93.6 2.1 %fusion.14 = f32[64,128,64]{1,2,0:T(8,128)} fusion(pred[64]{0:T(512)(128)(4,1)S(1)} %get-tuple-element.25, bf16[64,4,128,128]{3,2,1,0:T(8,128)(2,1)S(1)} %bitcast.220, bf16[8,64,8,128]{3,2,1,0:T(8,128)(2,1)S(1)} %get-tuple-element.8), kind=kOutput, calls=%fused_computation.25 | convolution fusion | flops 135266304 | bytes 5243392 | tf_op jit(solution)/shard_map/rcp,cpq->rcq/dot_general | solution.py:50
  95.7 2.1 %fusion.19 = f32[64,128,64]{1,2,0:T(8,128)} fusion(pred[64]{0:T(512)(128)(4,1)S(1)} %get-tuple-element.17, bf16[64,4,128,128]{3,2,1,0:T(8,128)(2,1)S(1)} %bitcast.220, bf16[8,64,8,128]{3,2,1,0:T(8,128)(2,1)S(1)} %get-tuple-element.8), kind=kOutput, calls=%fused_computation.35 | convolution fusion | flops 135266304 | bytes 5243392 | tf_op jit(solution)/shard_map/rcp,cpq->rcq/dot_general | solution.py:50
  97.8 2.1 %fusion.24 = f32[64,128,64]{1,2,0:T(8,128)} fusion(pred[64]{0:T(512)(128)(4,1)S(1)} %get-tuple-element.20, bf16[64,4,128,128]{3,2,1,0:T(8,128)(2,1)S(1)} %bitcast.220, bf16[8,64,8,128]{3,2,1,0:T(8,128)(2,1)S(1)} %get-tuple-element.7), kind=kOutput, calls=%fused_computation.49 | convolution fusion | flops 135266304 | bytes 5243392 | tf_op jit(solution)/shard_map/rcp,cpq->rcq/dot_general | solution.py:50
  99.9 2.1 %fusion.8 = f32[64,128,64]{1,2,0:T(8,128)} fusion(pred[64]{0:T(512)(128)(4,1)S(1)} %get-tuple-element.28, bf16[64,4,128,128]{3,2,1,0:T(8,128)(2,1)S(1)} %bitcast.220, bf16[8,64,8,128]{3,2,1,0:T(8,128)(2,1)S(1)} %get-tuple-element.7), kind=kOutput, calls=%fused_computation.14 | convolution fusion | flops 135266304 | bytes 5243392 | tf_op jit(solution)/shard_map/rcp,cpq->rcq/dot_general | solution.py:50
  102.0 0.0 copy-done.1
  102.0 2.1 %fusion.9 = f32[64,128,64]{1,2,0:T(8,128)} fusion(pred[64]{0:T(512)(128)(4,1)S(1)} %get-tuple-element.29, bf16[64,4,128,128]{3,2,1,0:T(8,128)(2,1)S(1)} %bitcast.220, bf16[8,64,8,128]{3,2,1,0:T(8,128)(2,1)S(1)} %get-tuple-element.8), kind=kOutput, calls=%fused_computation.15 | convolution fusion | flops 135266304 | bytes 5243392 | tf_op jit(solution)/shard_map/rcp,cpq->rcq/dot_general | solution.py:50
  104.1 2.1 %fusion.11 = f32[64,128,64]{1,2,0:T(8,128)} fusion(pred[64]{0:T(512)(128)(4,1)S(1)} %get-tuple-element.21, bf16[64,4,128,128]{3,2,1,0:T(8,128)(2,1)S(1)} %bitcast.220, bf16[8,64,8,128]{3,2,1,0:T(8,128)(2,1)S(1)} %get-tuple-element.6), kind=kOutput, calls=%fused_computation.22 | convolution fusion | flops 135266304 | bytes 5243392 | tf_op jit(solution)/shard_map/rcp,cpq->rcq/dot_general | solution.py:50
  106.2 2.1 %fusion.16 = f32[64,128,64]{1,2,0:T(8,128)} fusion(pred[64]{0:T(512)(128)(4,1)S(1)} %get-tuple-element.14, bf16[64,4,128,128]{3,2,1,0:T(8,128)(2,1)S(1)} %bitcast.220, bf16[8,64,8,128]{3,2,1,0:T(8,128)(2,1)S(1)} %get-tuple-element.6), kind=kOutput, calls=%fused_computation.32 | convolution fusion | flops 135266304 | bytes 5243392 | tf_op jit(solution)/shard_map/rcp,cpq->rcq/dot_general | solution.py:50
  108.3 0.0 copy-done.2
  108.3 2.0 %fusion.22 = f32[64,128,64]{1,2,0:T(8,128)} fusion(pred[64]{0:T(512)(128)(4,1)S(1)} %get-tuple-element.18, bf16[64,4,128,128]{3,2,1,0:T(8,128)(2,1)S(1)} %bitcast.220, bf16[8,64,8,128]{3,2,1,0:T(8,128)(2,1)S(1)} %get-tuple-element.6), kind=kOutput, calls=%fused_computation.47 | convolution fusion | flops 135266304 | bytes 5243392 | tf_op jit(solution)/shard_map/rcp,cpq->rcq/dot_general | solution.py:50
  110.4 2.1 %fusion.21 = f32[64,128,64]{1,2,0:T(8,128)} fusion(pred[64]{0:T(512)(128)(4,1)S(1)} %get-tuple-element.22, bf16[64,4,128,128]{3,2,1,0:T(8,128)(2,1)S(1)} %bitcast.220, bf16[8,64,8,128]{3,2,1,0:T(8,128)(2,1)S(1)} %get-tuple-element.5), kind=kOutput, calls=%fused_computation.46 | convolution fusion | flops 135266304 | bytes 5243392 | tf_op jit(solution)/shard_map/rcp,cpq->rcq/dot_general | solution.py:50
  112.5 2.0 %fusion.5 = f32[64,128,64]{1,2,0:T(8,128)} fusion(pred[64]{0:T(512)(128)(4,1)S(1)} %get-tuple-element.30, bf16[64,4,128,128]{3,2,1,0:T(8,128)(2,1)S(1)} %bitcast.220, bf16[8,64,8,128]{3,2,1,0:T(8,128)(2,1)S(1)} %get-tuple-element.5), kind=kOutput, calls=%fused_computation.11 | convolution fusion | flops 135266304 | bytes 5243392 | tf_op jit(solution)/shard_map/rcp,cpq->rcq/dot_general | solution.py:50
  114.5 13.9 %all-gather.2.cloned.1.call-done = bf16[16,16,64,128]{3,2,1,0:T(8,128)(2,1)} async-done(((bf16[4,16,64,128]{3,2,1,0:T(8,128)(2,1)}), bf16[16,16,64,128]{3,2,1,0:T(8,128)(2,1)}) %all-gather.2.cloned.1.call-update) | async-done | bytes 4194320 | tf_op jit(solution)/shard_map/all_gather | solution.py:54
  128.4 0.0 copy-done.6
  128.4 3.5 %fusion.48 = bf16[16,4,64,128]{3,2,0,1:T(8,128)(2,1)S(1)} fusion(bf16[16,16,64,128]{3,2,1,0:T(8,128)(2,1)} %all-gather.2.cloned.1.call-done, bf16[16,64,4,64,1]{3,2,1,0,4:T(4,128)(2,1)S(1)} %bitcast.221), kind=kOutput, calls=%fused_computation.72 | convolution fusion | flops 1074266112 | bytes 5767168 | tf_op jit(solution)/shard_map/ijba,jbkc->ikca/dot_general | solution.py:55
  131.8 1.0 copy.136
  132.9 3.7 %all-to-all-start.1 = ((bf16[16,4,64,128]{3,2,1,0:T(8,128)(2,1)}), bf16[16,4,64,128]{3,2,1,0:T(8,128)(2,1)S(1)}, u32[]{:S(2)}, u32[]{:S(2)}) async-start(bf16[16,4,64,128]{3,2,1,0:T(8,128)(2,1)} %copy.136), calls=%async_computation.1 | async-start | bytes 2097152 | tf_op jit(solution)/shard_map/all_to_all | solution.py:59
  136.6 4.0 %fusion.6 = f32[64,128,64]{1,2,0:T(8,128)} fusion(pred[64]{0:T(512)(128)(4,1)S(1)} %get-tuple-element.26, bf16[64,4,128,128]{3,2,1,0:T(8,128)(2,1)} %param.9, bf16[8,64,8,128]{3,2,1,0:T(8,128)(2,1)} %copy-done.2), kind=kOutput, calls=%fused_computation.12 | convolution fusion | flops 135266304 | bytes 5242944 | tf_op jit(solution)/shard_map/rcp,cpq->rcq/dot_general | solution.py:50
  140.7 3.6 %fusion.10 = f32[64,128,64]{1,2,0:T(8,128)} fusion(pred[64]{0:T(512)(128)(4,1)S(1)} %get-tuple-element.32, bf16[64,4,128,128]{3,2,1,0:T(8,128)(2,1)} %param.9, bf16[8,64,8,128]{3,2,1,0:T(8,128)(2,1)S(1)} %get-tuple-element.5), kind=kOutput, calls=%fused_computation.21 | convolution fusion | flops 135266304 | bytes 5242944 | tf_op jit(solution)/shard_map/rcp,cpq->rcq/dot_general | solution.py:50
  144.3 3.6 %fusion.15 = f32[64,128,64]{1,2,0:T(8,128)} fusion(pred[64]{0:T(512)(128)(4,1)S(1)} %get-tuple-element.31, bf16[64,4,128,128]{3,2,1,0:T(8,128)(2,1)} %param.9, bf16[8,64,8,128]{3,2,1,0:T(8,128)(2,1)S(1)} %get-tuple-element.5), kind=kOutput, calls=%fused_computation.31 | convolution fusion | flops 135266304 | bytes 5242944 | tf_op jit(solution)/shard_map/rcp,cpq->rcq/dot_general | solution.py:50
  147.9 2.9 %all-to-all-done.1 = bf16[16,4,64,128]{3,2,1,0:T(8,128)(2,1)S(1)} async-done(((bf16[16,4,64,128]{3,2,1,0:T(8,128)(2,1)}), bf16[16,4,64,128]{3,2,1,0:T(8,128)(2,1)S(1)}, u32[]{:S(2)}, u32[]{:S(2)}) %all-to-all-start.1) | async-done | bytes 1048608 | tf_op jit(solution)/shard_map/all_to_all | solution.py:59
  150.9 0.1 copy.137
  151.0 1.6 copy.138
  152.6 8.6 %all-to-all-start.2 = ((bf16[4,16,64,128]{3,1,0,2:T(8,128)(2,1)}), bf16[4,16,64,128]{3,1,0,2:T(8,128)(2,1)}, u32[]{:S(2)}, u32[]{:S(2)}) async-start(bf16[4,16,64,128]{3,1,0,2:T(8,128)(2,1)} %copy.138), calls=%async_computation.2 | async-start | bytes 2097152 | tf_op jit(solution)/shard_map/all_to_all | solution.py:58
  161.3 15.6 %fusion.20 = f32[64,8,8,128]{3,2,1,0:T(8,128)S(1)} fusion(f32[64,128,64]{1,2,0:T(8,128)} %fusion.9, f32[64,128,64]{1,2,0:T(8,128)} %fusion.14, f32[64,128,64]{1,2,0:T(8,128)} %fusion.19, f32[64,128,64]{1,2,0:T(8,128)} %fusion.8, f32[64,128,64]{1,2,0:T(8,128)} %fusion.13, f32[64,128,64]{1,2,0:T(8,128)} %fusion.24, f32[64,128,64]{1,2,0:T(8,128)} %fusion.18, ...), kind=kOutput, calls=%fused_computation.38 | convolution fusion | flops 145227776 | bytes 45088832 | tf_op jit(solution)/shard_map/rcp,cpq->rcq/dot_general | solution.py:50
  176.9 1.4 all-to-all-done.2
  178.2 1.4 copy.139
  179.6 0.3 convert_bitcast_fusion
  179.9 2.6 %copy.140 = f32[4,16,2,32,128]{4,3,2,1,0:T(8,128)} copy(f32[4,16,2,32,128]{4,1,2,3,0:T(8,128)S(1)} %convert_bitcast_fusion) | data formatting | bytes 4194304 | tf_op jit(solution)/shard_map/convert_element_type | solution.py:68
  182.5 2.7 %reshape.301 = f32[64,8192]{1,0:T(8,128)} reshape(f32[4,16,2,32,128]{4,3,2,1,0:T(8,128)} %copy.140) | data formatting | bytes 4194304 | tf_op jit(solution)/shard_map/convert_element_type | solution.py:68
  185.2 0.0 copy-done.5
  185.2 3.1 %fusion.4 = bf16[64,8192]{1,0:T(8,128)(2,1)} fusion(f32[64,8192]{1,0:T(8,128)} %reshape.301, f32[64,8,8,128]{3,2,1,0:T(8,128)S(1)} %fusion.20, bf16[64,8192]{1,0:T(8,128)(2,1)S(1)} %copy-done, f32[8192]{0:T(1024)S(1)} %copy-done.3, f32[64]{0:T(128)S(1)} %copy-done.5), kind=kLoop, calls=%fused_computation.5 | loop fusion | flops 3145728 | bytes 6324480 | tf_op jit(solution)/shard_map/convert_element_type | solution.py:70
  (16 shorter events, 0.1 us)
Async XLA Ops:
  7.3 79.0 %collective-permute-start = (bf16[64,256]{1,0:T(8,128)(2,1)S(1)}, bf16[64,256]{1,0:T(8,128)(2,1)S(1)}, u32[]{:S(2)}, u32[]{:S(2)}) collective-permute-start(bf16[64,256]{1,0:T(8,128)(2,1)S(1)} %get-tuple-element.11), channel_id=1, source_target_pairs={{0,1},{1,2},{2,3},{3,4},{4,5},{5,6},{6,7},{7,8},{8,9},{9,10},{10,1... | collective-permute-start | bytes 98312 | tf_op jit(solution)/shard_map/ppermute | solution.py:19
  12.2 74.3 %collective-permute-start.1 = (bf16[64,256]{1,0:T(8,128)(2,1)S(1)}, bf16[64,256]{1,0:T(8,128)(2,1)S(1)}, u32[]{:S(2)}, u32[]{:S(2)}) collective-permute-start(bf16[64,256]{1,0:T(8,128)(2,1)S(1)} %get-tuple-element.12), channel_id=1, source_target_pairs={{1,0},{2,1},{3,2},{4,3},{5,4},{6,5},{7,6},{8,7},{9,8},{10,9},{11,1... | collective-permute-start | bytes 98312 | tf_op jit(solution)/shard_map/ppermute | solution.py:22
  36.7 8.5 %copy-start.7 = (s32[64]{0:T(128)S(1)}, s32[64]{0:T(128)}, u32[]{:S(2)}) copy-start(s32[64]{0:T(128)} %param.11) | copy-start | bytes 772
  36.7 8.5 %copy-start.4 = (s32[64,4]{0,1:T(4,128)S(1)}, s32[64,4]{0,1:T(4,128)}, u32[]{:S(2)}) copy-start(s32[64,4]{0,1:T(4,128)} %param.10) | copy-start | bytes 3076
  36.7 8.6 %copy-start = (bf16[64,8192]{1,0:T(8,128)(2,1)S(1)}, bf16[64,8192]{1,0:T(8,128)(2,1)}, u32[]{:S(2)}) copy-start(bf16[64,8192]{1,0:T(8,128)(2,1)} %param.7) | copy-start | bytes 3145732
  36.7 25.4 %all-to-all-start = ((bf16[32,2,8192]{2,1,0:T(2,128)(2,1)}), bf16[32,2,8192]{2,1,0:T(2,128)(2,1)S(1)}, u32[]{:S(2)}, u32[]{:S(2)}) async-start(bf16[32,2,8192]{2,1,0:T(2,128)(2,1)} %reshape.306), calls=%async_computation | async-start | bytes 2097152 | tf_op jit(solution)/shard_map/all_to_all | solution.py:34
  45.1 83.3 %all-gather.2.cloned.1.call-start = ((), (), s32[]{:S(2)}) async-start(), calls=%async_computation.3 | async-start | bytes 5242880 | tf_op jit(solution)/shard_map/all_gather | solution.py:54
  82.4 4.8 %slice-start = ((s8[8388608]{0:T(1024)(128)(4,1)}), s8[4194304]{0:T(1024)(128)(4,1)S(1)}, s32[]{:S(2)}) async-start(s8[8388608]{0:T(1024)(128)(4,1)} %bitcast.219), calls=%async_computation.4 | async-start | bytes 8388608
  86.3 3.1 %slice-start.1 = ((s8[8388608]{0:T(1024)(128)(4,1)}), s8[4194304]{0:T(1024)(128)(4,1)S(1)}, s32[]{:S(2)}) async-start(s8[8388608]{0:T(1024)(128)(4,1)} %bitcast.219), calls=%async_computation.5 | async-start | bytes 8388608
  86.9 15.1 %copy-start.1 = (bf16[8,64,8,128]{3,2,1,0:T(8,128)(2,1)}, bf16[8,64,8,128]{3,2,1,0:T(8,128)(2,1)S(1)}, u32[]{:S(2)}) copy-start(bf16[8,64,8,128]{3,2,1,0:T(8,128)(2,1)S(1)} %get-tuple-element.8) | copy-start | bytes 3145732
  87.2 21.1 %copy-start.2 = (bf16[8,64,8,128]{3,2,1,0:T(8,128)(2,1)}, bf16[8,64,8,128]{3,2,1,0:T(8,128)(2,1)S(1)}, u32[]{:S(2)}) copy-start(bf16[8,64,8,128]{3,2,1,0:T(8,128)(2,1)S(1)} %get-tuple-element.6) | copy-start | bytes 3145732
  112.5 15.9 %copy-start.6 = (bf16[16,64,4,64]{3,2,1,0:T(4,128)(2,1)S(1)}, bf16[16,64,4,64]{3,2,1,0:T(4,128)(2,1)}, u32[]{:S(2)}) copy-start(bf16[16,64,4,64]{3,2,1,0:T(4,128)(2,1)} %param.8) | copy-start | bytes 1572868
  132.9 18.0 %all-to-all-start.1 = ((bf16[16,4,64,128]{3,2,1,0:T(8,128)(2,1)}), bf16[16,4,64,128]{3,2,1,0:T(8,128)(2,1)S(1)}, u32[]{:S(2)}, u32[]{:S(2)}) async-start(bf16[16,4,64,128]{3,2,1,0:T(8,128)(2,1)} %copy.136), calls=%async_computation.1 | async-start | bytes 2097152 | tf_op jit(solution)/shard_map/all_to_all | solution.py:59
  152.6 25.6 %all-to-all-start.2 = ((bf16[4,16,64,128]{3,1,0,2:T(8,128)(2,1)}), bf16[4,16,64,128]{3,1,0,2:T(8,128)(2,1)}, u32[]{:S(2)}, u32[]{:S(2)}) async-start(bf16[4,16,64,128]{3,1,0,2:T(8,128)(2,1)} %copy.138), calls=%async_computation.2 | async-start | bytes 2097152 | tf_op jit(solution)/shard_map/all_to_all | solution.py:58
  182.5 2.7 %copy-start.3 = (f32[8192]{0:T(1024)S(1)}, f32[8192]{0:T(1024)}, u32[]{:S(2)}) copy-start(f32[8192]{0:T(1024)} %param.13) | copy-start | bytes 98308
  182.5 2.7 %copy-start.5 = (f32[64]{0:T(128)S(1)}, f32[64]{0:T(128)}, u32[]{:S(2)}) copy-start(f32[64]{0:T(128)} %param.12) | copy-start | bytes 772
Sparse Core Ops, SparseCore 0:
  82.6 45.7 all-gather.1
where the time goes:
time: 196 us; the launch traced here: 195 us
  matrix products  70.3 us (36%)
  local copies, waits for them, and re-layouts  56.1 us (29%)
  starting transfers between devices  27.7 us (14%)
  waiting for transfers between devices  23.9 us (12%)
  between operations  13.7 us (7%)
  other arithmetic  3.39 us (2%)
    dot_general x20, matrix products, local(): jnp.einsum('rcp,cpq->rcq', window, masked, preferred_element_type=jnp.flo...  66.9 us
    unnamed x25, local copies, waits for them, and re-layouts  21.7 us
    all_gather x1, waiting for transfers between devices, local(): all_rows = lax.all_gather(cycle_input, 'occ', axis=0, tiled=True)  13.9 us
    all_to_all x1, local copies, waits for them, and re-layouts, local(): lax.all_to_all(four_dim, 'vir', split_axis=3, concat_axis=2, tiled=True)  12.8 us
    reshape x2, local copies, waits for them, and re-layouts, local(): four_dim = amplitudes.reshape(outer_occ, NJ, NB_DEV, NA)  11.3 us
    all_to_all x1, starting transfers between devices, local(): lax.all_to_all(lax.all_to_all(cycle_part, 'occ', split_axis=0, concat_axi...  8.64 us
    all_to_all x1, starting transfers between devices, local(): lax.all_to_all(four_dim, 'vir', split_axis=3, concat_axis=2, tiled=True)  8.45 us
    all_to_all x1, waiting for transfers between devices, local(): lax.all_to_all(four_dim, 'vir', split_axis=3, concat_axis=2, tiled=True)  5.69 us
  transfers between devices with their start and end apart: 6, of which 4 were waited for; matrix products, arithmetic and copies ran while one was open for 57% of the time, Pallas kernels for 0%

commit v1 on v0

--- a/solution.py
+++ b/solution.py
@@ -51,7 +51,9 @@
                 "rcp,cpq->rcq", window, masked, preferred_element_type=jnp.float32
             )
     ladder = ladder.reshape(rows_dev, cols_dev)
-    all_rows = lax.all_gather(cycle_input, "occ", axis=0, tiled=True)
+    spare = tuple((cycle_input for _ in range(lax.axis_size("occ"))))
+    even = jnp.concatenate(spare, axis=0)
+    all_rows = lax.all_to_all(even, "occ", 0, 0, tiled=True)
     cycle_part = jnp.einsum(
         "ijba,jbkc->ikca", all_rows, cycle_integrals, preferred_element_type=jnp.float32
     ).astype(jnp.bfloat16)

time: 196 us -> 205 us (1.046)
  between operations: 13.7 us -> 0.27 us
  matrix products: 70.3 us -> 80.7 us
  waiting for transfers between devices: 23.9 us -> 29.5 us
  starting transfers between devices: 27.7 us -> 32.8 us
  other arithmetic: 3.39 us -> 5.67 us
    all_to_all x0 -> x1, waiting for transfers between devices: none -> 25.5 us  [local(): all_rows = lax.all_to_all(even, 'occ', 0, 0, tiled=True)]
    all_gather x1 -> x0, waiting for transfers between devices: 13.9 us -> none  [local(): all_rows = lax.all_gather(cycle_input, 'occ', axis=0, tiled=True)]
    dot_general x20, matrix products: 66.9 us -> 76.3 us  [local(): jnp.einsum('rcp,cpq->rcq', window, masked, preferred_element_type=jnp.flo...]
    all_to_all x1, waiting for transfers between devices: 5.69 us -> 0.01 us  [local(): lax.all_to_all(four_dim, 'vir', split_axis=3, concat_axis=2, tiled=True)]
    all_to_all x0 -> x1, starting transfers between devices: none -> 5.03 us  [local(): all_rows = lax.all_to_all(even, 'occ', 0, 0, tiled=True)]
    concatenate x0 -> x1, other arithmetic: none -> 2.28 us  [local(): even = jnp.concatenate(spare, axis=0)]
    unnamed x25 -> x38, local copies, waits for them, and re-layouts: 21.7 us -> 21.9 us
  transfers between devices with their start and end apart: 6 -> 6, of which waited for: 4 -> 3; matrix products, arithmetic and copies ran while one was open for 57% -> 50% of each run, Pallas kernels for 0% -> 0%
where the time goes in v1:
time: 205 us; the launch traced here: 203 us
  matrix products  80.7 us (39%)
  local copies, waits for them, and re-layouts  54.4 us (27%)
  starting transfers between devices  32.8 us (16%)
  waiting for transfers between devices  29.5 us (14%)
  other arithmetic  5.67 us (3%)
    dot_general x20, matrix products, local(): jnp.einsum('rcp,cpq->rcq', window, masked, preferred_element_type=jnp.flo...  76.3 us
    all_to_all x1, waiting for transfers between devices, local(): all_rows = lax.all_to_all(even, 'occ', 0, 0, tiled=True)  25.5 us
    unnamed x38, local copies, waits for them, and re-layouts  21.9 us
    all_to_all x1, local copies, waits for them, and re-layouts, local(): lax.all_to_all(four_dim, 'vir', split_axis=3, concat_axis=2, tiled=True)  11.9 us
    reshape x2, local copies, waits for them, and re-layouts, local(): four_dim = amplitudes.reshape(outer_occ, NJ, NB_DEV, NA)  11.2 us
    all_to_all x1, starting transfers between devices, local(): lax.all_to_all(lax.all_to_all(cycle_part, 'occ', split_axis=0, concat_axi...  8.93 us
    all_to_all x1, starting transfers between devices, local(): lax.all_to_all(four_dim, 'vir', split_axis=3, concat_axis=2, tiled=True)  8.45 us
    convert_element_type x2, local copies, waits for them, and re-layouts, local(): cycle_flat.astype(jnp.float32) + ladder  5.31 us
  transfers between devices with their start and end apart: 6, of which 3 were waited for; matrix products, arithmetic and copies ran while one was open for 50% of the time, Pallas kernels for 0%

profile of v1, /device:TPU:1, one launch (start us, length us, event | category | flops | bytes accessed | tf_op | source)
XLA Modules:
  0.0 203.4 jit_solution(13714625920768086906)
XLA Ops:
  0.0 0.8 fusion.152
  0.8 4.9 %collective-permute-start = (bf16[64,256]{1,0:T(8,128)(2,1)S(1)}, bf16[64,256]{1,0:T(8,128)(2,1)S(1)}, u32[]{:S(2)}, u32[]{:S(2)}) collective-permute-start(bf16[64,256]{1,0:T(8,128)(2,1)S(1)} %get-tuple-element.11), channel_id=1, source_target_pairs={{0,1},{1,2},{2,3},{3,4},{4,5},{5,6},{6,7},{7,8},{8,9},{9,10},{10,1... | collective-permute-start | bytes 98312 | tf_op jit(solution)/shard_map/ppermute | solution.py:19
  5.7 1.9 collective-permute-start.1
  7.6 1.8 reshape.294
  9.5 9.4 %copy.132 = bf16[4,16,2,4096]{1,0,2,3:T(4,128)(2,1)} copy(bf16[4,16,2,4096]{3,2,1,0:T(2,128)(2,1)S(1)} %reshape.294) | data formatting | bytes 2097152 | tf_op jit(solution)/shard_map/reshape | solution.py:33
  18.9 11.2 %reshape.306 = bf16[32,2,8192]{2,1,0:T(2,128)(2,1)} reshape(bf16[4096,2,4,16]{3,2,1,0:T(4,128)(2,1)} %bitcast.217) | data formatting | bytes 2097152
  30.1 8.4 %all-to-all-start = ((bf16[32,2,8192]{2,1,0:T(2,128)(2,1)}), bf16[32,2,8192]{2,1,0:T(2,128)(2,1)S(1)}, u32[]{:S(2)}, u32[]{:S(2)}) async-start(bf16[32,2,8192]{2,1,0:T(2,128)(2,1)} %reshape.306), calls=%async_computation | async-start | bytes 2097152 | tf_op jit(solution)/shard_map/all_to_all | solution.py:34
  38.6 0.0 copy-done.11
  38.6 0.0 copy-done.9
  38.6 0.0 copy-done
  38.7 3.7 %fusion.12 = f32[64,128,64]{1,2,0:T(8,128)} fusion(pred[64]{0:T(512)(128)(4,1)S(1)} %get-tuple-element.23, bf16[64,4,128,128]{3,2,1,0:T(8,128)(2,1)} %param.9, bf16[64,8192]{1,0:T(8,128)(2,1)S(1)} %copy-done), kind=kOutput, calls=%fused_computation.24 | convolution fusion | flops 135266304 | bytes 5242944 | tf_op jit(solution)/shard_map/rcp,cpq->rcq/dot_general | solution.py:50
  42.4 3.6 %fusion.17 = f32[64,128,64]{1,2,0:T(8,128)} fusion(pred[64]{0:T(512)(128)(4,1)S(1)} %get-tuple-element.15, bf16[64,4,128,128]{3,2,1,0:T(8,128)(2,1)} %param.9, bf16[64,8192]{1,0:T(8,128)(2,1)S(1)} %copy-done), kind=kOutput, calls=%fused_computation.34 | convolution fusion | flops 135266304 | bytes 5242944 | tf_op jit(solution)/shard_map/rcp,cpq->rcq/dot_general | solution.py:50
  46.0 3.7 %fusion.23 = f32[64,128,64]{1,2,0:T(8,128)} fusion(pred[64]{0:T(512)(128)(4,1)S(1)} %get-tuple-element.19, bf16[64,4,128,128]{3,2,1,0:T(8,128)(2,1)} %param.9, bf16[64,8192]{1,0:T(8,128)(2,1)S(1)} %copy-done), kind=kOutput, calls=%fused_computation.49 | convolution fusion | flops 135266304 | bytes 5242944 | tf_op jit(solution)/shard_map/rcp,cpq->rcq/dot_general | solution.py:50
  49.7 3.8 %fusion.7 = f32[64,128,64]{1,2,0:T(8,128)} fusion(pred[64]{0:T(512)(128)(4,1)S(1)} %get-tuple-element.27, bf16[64,4,128,128]{3,2,1,0:T(8,128)(2,1)} %param.9, bf16[64,8192]{1,0:T(8,128)(2,1)S(1)} %copy-done), kind=kOutput, calls=%fused_computation.14 | convolution fusion | flops 135266304 | bytes 5242944 | tf_op jit(solution)/shard_map/rcp,cpq->rcq/dot_general | solution.py:50
  53.5 0.0 copy-done.3
  53.5 1.5 copy.134
  55.0 0.0 collective-permute-done
  55.0 0.1 constant_dynamic-update-slice_fusion
  55.1 0.0 collective-permute-done.1
  55.2 0.0 slice-start
  55.2 0.4 slice_bitcast_fusion.1
  55.5 0.0 copy-start.5
  55.6 0.0 copy-start.1
  55.6 0.0 slice-start.1
  55.6 4.7 %fusion.13 = f32[64,128,64]{1,2,0:T(8,128)} fusion(pred[64]{0:T(512)(128)(4,1)S(1)} %get-tuple-element.24, bf16[64,4,128,128]{3,2,1,0:T(8,128)(2,1)} %param.9, bf16[8,64,8,128]{3,2,1,0:T(8,128)(2,1)S(1)} %get-tuple-element.7), kind=kOutput, calls=%fused_computation.25 | convolution fusion | flops 135266304 | bytes 5242944 | tf_op jit(solution)/shard_map/rcp,cpq->rcq/dot_general | solution.py:50
  60.3 0.0 copy-done.5
  60.3 3.8 %fusion.18 = f32[64,128,64]{1,2,0:T(8,128)} fusion(pred[64]{0:T(512)(128)(4,1)S(1)} %get-tuple-element.16, bf16[64,4,128,128]{3,2,1,0:T(8,128)(2,1)} %param.9, bf16[8,64,8,128]{3,2,1,0:T(8,128)(2,1)S(1)} %get-tuple-element.7), kind=kOutput, calls=%fused_computation.35 | convolution fusion | flops 135266304 | bytes 5242944 | tf_op jit(solution)/shard_map/rcp,cpq->rcq/dot_general | solution.py:50
  64.0 0.0 slice-done
  64.0 2.1 %fusion.14 = f32[64,128,64]{1,2,0:T(8,128)} fusion(pred[64]{0:T(512)(128)(4,1)S(1)} %get-tuple-element.25, bf16[64,4,128,128]{3,2,1,0:T(8,128)(2,1)S(1)} %bitcast.224, bf16[8,64,8,128]{3,2,1,0:T(8,128)(2,1)S(1)} %get-tuple-element.8), kind=kOutput, calls=%fused_computation.26 | convolution fusion | flops 135266304 | bytes 5243392 | tf_op jit(solution)/shard_map/rcp,cpq->rcq/dot_general | solution.py:50
  66.1 2.1 %fusion.19 = f32[64,128,64]{1,2,0:T(8,128)} fusion(pred[64]{0:T(512)(128)(4,1)S(1)} %get-tuple-element.17, bf16[64,4,128,128]{3,2,1,0:T(8,128)(2,1)S(1)} %bitcast.224, bf16[8,64,8,128]{3,2,1,0:T(8,128)(2,1)S(1)} %get-tuple-element.8), kind=kOutput, calls=%fused_computation.36 | convolution fusion | flops 135266304 | bytes 5243392 | tf_op jit(solution)/shard_map/rcp,cpq->rcq/dot_general | solution.py:50
  68.2 0.0 all-to-all-done
  68.2 7.6 %reshape.307 = bf16[4096,2,4,16]{3,2,1,0:T(4,128)(2,1)} reshape(bf16[32,2,8192]{2,1,0:T(2,128)(2,1)S(1)} %all-to-all-done) | data formatting | bytes 2097152
  75.8 11.9 %copy.133 = bf16[4,16,2,32,128]{4,2,3,1,0:T(2,128)(2,1)S(1)} copy(bf16[4,16,2,32,128]{1,0,2,4,3:T(4,128)(2,1)} %bitcast.218) | data formatting | bytes 2097152 | tf_op jit(solution)/shard_map/all_to_all | solution.py:34
  87.8 2.3 %pad_maximum_fusion = bf16[16,16,64,128]{3,2,1,0:T(8,128)(2,1)} fusion(bf16[4,16,64,128]{3,2,1,0:T(8,128)(2,1)S(1)} %bitcast.219), kind=kLoop, calls=%fused_computation | loop fusion | flops 6291456 | bytes 5242880 | tf_op jit(solution)/shard_map/concatenate | solution.py:55
  90.0 5.0 %all-to-all-start.1 = ((bf16[16,16,64,128]{3,2,1,0:T(8,128)(2,1)}), bf16[16,16,64,128]{3,2,1,0:T(8,128)(2,1)}, u32[]{:S(2)}, u32[]{:S(2)}) async-start(bf16[16,16,64,128]{3,2,1,0:T(8,128)(2,1)} %pad_maximum_fusion), calls=%async_computation.1 | async-start | bytes 8388608 | tf_op jit(solution)/shard_map/all_to_all | solution.py:56
  95.1 0.3 slice_bitcast_fusion.3
  95.4 0.0 copy-start.7
  95.4 0.9 copy-done.6
  96.3 3.8 %fusion.24 = f32[64,128,64]{1,2,0:T(8,128)} fusion(pred[64]{0:T(512)(128)(4,1)S(1)} %get-tuple-element.20, bf16[64,4,128,128]{3,2,1,0:T(8,128)(2,1)} %param.9, bf16[8,64,8,128]{3,2,1,0:T(8,128)(2,1)S(1)} %copy-done.6), kind=kOutput, calls=%fused_computation.50 | convolution fusion | flops 135266304 | bytes 5242944 | tf_op jit(solution)/shard_map/rcp,cpq->rcq/dot_general | solution.py:50
  100.1 3.9 %fusion.8 = f32[64,128,64]{1,2,0:T(8,128)} fusion(pred[64]{0:T(512)(128)(4,1)S(1)} %get-tuple-element.28, bf16[64,4,128,128]{3,2,1,0:T(8,128)(2,1)} %param.9, bf16[8,64,8,128]{3,2,1,0:T(8,128)(2,1)S(1)} %copy-done.6), kind=kOutput, calls=%fused_computation.15 | convolution fusion | flops 135266304 | bytes 5242944 | tf_op jit(solution)/shard_map/rcp,cpq->rcq/dot_general | solution.py:50
  104.0 3.7 %fusion.9 = f32[64,128,64]{1,2,0:T(8,128)} fusion(pred[64]{0:T(512)(128)(4,1)S(1)} %get-tuple-element.29, bf16[64,4,128,128]{3,2,1,0:T(8,128)(2,1)} %param.9, bf16[8,64,8,128]{3,2,1,0:T(8,128)(2,1)S(1)} %copy-done.2), kind=kOutput, calls=%fused_computation.16 | convolution fusion | flops 135266304 | bytes 5242944 | tf_op jit(solution)/shard_map/rcp,cpq->rcq/dot_general | solution.py:50
  107.7 2.1 %fusion.11 = f32[64,128,64]{1,2,0:T(8,128)} fusion(pred[64]{0:T(512)(128)(4,1)S(1)} %get-tuple-element.21, bf16[64,4,128,128]{3,2,1,0:T(8,128)(2,1)S(1)} %bitcast.226, bf16[8,64,8,128]{3,2,1,0:T(8,128)(2,1)S(1)} %get-tuple-element.6), kind=kOutput, calls=%fused_computation.23 | convolution fusion | flops 135266304 | bytes 5243392 | tf_op jit(solution)/shard_map/rcp,cpq->rcq/dot_general | solution.py:50
  109.8 2.1 %fusion.16 = f32[64,128,64]{1,2,0:T(8,128)} fusion(pred[64]{0:T(512)(128)(4,1)S(1)} %get-tuple-element.14, bf16[64,4,128,128]{3,2,1,0:T(8,128)(2,1)S(1)} %bitcast.226, bf16[8,64,8,128]{3,2,1,0:T(8,128)(2,1)S(1)} %get-tuple-element.6), kind=kOutput, calls=%fused_computation.33 | convolution fusion | flops 135266304 | bytes 5243392 | tf_op jit(solution)/shard_map/rcp,cpq->rcq/dot_general | solution.py:50
  111.9 2.1 %fusion.22 = f32[64,128,64]{1,2,0:T(8,128)} fusion(pred[64]{0:T(512)(128)(4,1)S(1)} %get-tuple-element.18, bf16[64,4,128,128]{3,2,1,0:T(8,128)(2,1)S(1)} %bitcast.226, bf16[8,64,8,128]{3,2,1,0:T(8,128)(2,1)S(1)} %get-tuple-element.6), kind=kOutput, calls=%fused_computation.48 | convolution fusion | flops 135266304 | bytes 5243392 | tf_op jit(solution)/shard_map/rcp,cpq->rcq/dot_general | solution.py:50
  113.9 2.1 %fusion.21 = f32[64,128,64]{1,2,0:T(8,128)} fusion(pred[64]{0:T(512)(128)(4,1)S(1)} %get-tuple-element.22, bf16[64,4,128,128]{3,2,1,0:T(8,128)(2,1)S(1)} %bitcast.226, bf16[8,64,8,128]{3,2,1,0:T(8,128)(2,1)S(1)} %get-tuple-element.5), kind=kOutput, calls=%fused_computation.47 | convolution fusion | flops 135266304 | bytes 5243392 | tf_op jit(solution)/shard_map/rcp,cpq->rcq/dot_general | solution.py:50
  116.1 2.0 %fusion.5 = f32[64,128,64]{1,2,0:T(8,128)} fusion(pred[64]{0:T(512)(128)(4,1)S(1)} %get-tuple-element.30, bf16[64,4,128,128]{3,2,1,0:T(8,128)(2,1)S(1)} %bitcast.226, bf16[8,64,8,128]{3,2,1,0:T(8,128)(2,1)S(1)} %get-tuple-element.5), kind=kOutput, calls=%fused_computation.12 | convolution fusion | flops 135266304 | bytes 5243392 | tf_op jit(solution)/shard_map/rcp,cpq->rcq/dot_general | solution.py:50
  118.1 25.5 %all-to-all-done.1 = bf16[16,16,64,128]{3,2,1,0:T(8,128)(2,1)} async-done(((bf16[16,16,64,128]{3,2,1,0:T(8,128)(2,1)}), bf16[16,16,64,128]{3,2,1,0:T(8,128)(2,1)}, u32[]{:S(2)}, u32[]{:S(2)}) %all-to-all-start.1) | async-done | bytes 4194336 | tf_op jit(solution)/shard_map/all_to_all | solution.py:56
  143.7 0.0 copy-done.4
  143.7 4.5 %fusion.48 = bf16[16,4,64,128]{3,2,1,0:T(8,128)(2,1)} fusion(bf16[16,16,64,128]{3,2,1,0:T(8,128)(2,1)} %all-to-all-done.1, bf16[16,64,4,64]{1,3,0,2:T(8,128)(2,1)S(1)} %copy-done.4), kind=kOutput, calls=%fused_computation.73 | convolution fusion | flops 1074266112 | bytes 5767168 | tf_op jit(solution)/shard_map/ijba,jbkc->ikca/dot_general | solution.py:57
  148.1 3.5 %all-to-all-start.2 = ((bf16[16,4,64,128]{3,2,1,0:T(8,128)(2,1)}), bf16[16,4,64,128]{3,2,1,0:T(8,128)(2,1)S(1)}, u32[]{:S(2)}, u32[]{:S(2)}) async-start(bf16[16,4,64,128]{3,2,1,0:T(8,128)(2,1)} %fusion.48), calls=%async_computation.2 | async-start | bytes 2097152 | tf_op jit(solution)/shard_map/all_to_all | solution.py:61
  151.6 4.0 %fusion.6 = f32[64,128,64]{1,2,0:T(8,128)} fusion(pred[64]{0:T(512)(128)(4,1)S(1)} %get-tuple-element.26, bf16[64,4,128,128]{3,2,1,0:T(8,128)(2,1)} %param.9, bf16[8,64,8,128]{3,2,1,0:T(8,128)(2,1)} %copy-done.7), kind=kOutput, calls=%fused_computation.13 | convolution fusion | flops 135266304 | bytes 5242944 | tf_op jit(solution)/shard_map/rcp,cpq->rcq/dot_general | solution.py:50
  155.7 3.7 %fusion.10 = f32[64,128,64]{1,2,0:T(8,128)} fusion(pred[64]{0:T(512)(128)(4,1)S(1)} %get-tuple-element.32, bf16[64,4,128,128]{3,2,1,0:T(8,128)(2,1)} %param.9, bf16[8,64,8,128]{3,2,1,0:T(8,128)(2,1)S(1)} %get-tuple-element.5), kind=kOutput, calls=%fused_computation.22 | convolution fusion | flops 135266304 | bytes 5242944 | tf_op jit(solution)/shard_map/rcp,cpq->rcq/dot_general | solution.py:50
  159.3 3.7 %fusion.15 = f32[64,128,64]{1,2,0:T(8,128)} fusion(pred[64]{0:T(512)(128)(4,1)S(1)} %get-tuple-element.31, bf16[64,4,128,128]{3,2,1,0:T(8,128)(2,1)} %param.9, bf16[8,64,8,128]{3,2,1,0:T(8,128)(2,1)S(1)} %get-tuple-element.5), kind=kOutput, calls=%fused_computation.32 | convolution fusion | flops 135266304 | bytes 5242944 | tf_op jit(solution)/shard_map/rcp,cpq->rcq/dot_general | solution.py:50
  163.1 2.6 %all-to-all-done.2 = bf16[16,4,64,128]{3,2,1,0:T(8,128)(2,1)S(1)} async-done(((bf16[16,4,64,128]{3,2,1,0:T(8,128)(2,1)}), bf16[16,4,64,128]{3,2,1,0:T(8,128)(2,1)S(1)}, u32[]{:S(2)}, u32[]{:S(2)}) %all-to-all-start.2) | async-done | bytes 1048608 | tf_op jit(solution)/shard_map/all_to_all | solution.py:61
  165.7 0.1 copy.135
  165.8 1.6 copy.136
  167.4 8.9 %all-to-all-start.3 = ((bf16[4,16,64,128]{3,1,0,2:T(8,128)(2,1)}), bf16[4,16,64,128]{3,1,0,2:T(8,128)(2,1)}, u32[]{:S(2)}, u32[]{:S(2)}) async-start(bf16[4,16,64,128]{3,1,0,2:T(8,128)(2,1)} %copy.136), calls=%async_computation.3 | async-start | bytes 2097152 | tf_op jit(solution)/shard_map/all_to_all | solution.py:60
  176.4 15.6 %fusion.20 = f32[64,8,8,128]{3,2,1,0:T(8,128)S(1)} fusion(f32[64,128,64]{1,2,0:T(8,128)} %fusion.9, f32[64,128,64]{1,2,0:T(8,128)} %fusion.14, f32[64,128,64]{1,2,0:T(8,128)} %fusion.19, f32[64,128,64]{1,2,0:T(8,128)} %fusion.8, f32[64,128,64]{1,2,0:T(8,128)} %fusion.13, f32[64,128,64]{1,2,0:T(8,128)} %fusion.24, f32[64,128,64]{1,2,0:T(8,128)} %fusion.18, ...), kind=kOutput, calls=%fused_computation.39 | convolution fusion | flops 145227776 | bytes 45088832 | tf_op jit(solution)/shard_map/rcp,cpq->rcq/dot_general | solution.py:50
  192.0 1.3 all-to-all-done.3
  193.3 1.4 copy.137
  194.7 0.3 convert_bitcast_fusion
  195.0 2.6 %copy.138 = f32[4,16,2,32,128]{4,3,2,1,0:T(8,128)} copy(f32[4,16,2,32,128]{4,1,2,3,0:T(8,128)S(1)} %convert_bitcast_fusion) | data formatting | bytes 4194304 | tf_op jit(solution)/shard_map/convert_element_type | solution.py:70
  197.6 2.7 %reshape.301 = f32[64,8192]{1,0:T(8,128)} reshape(f32[4,16,2,32,128]{4,3,2,1,0:T(8,128)} %copy.138) | data formatting | bytes 4194304 | tf_op jit(solution)/shard_map/convert_element_type | solution.py:70
  200.3 3.1 %fusion.4 = bf16[64,8192]{1,0:T(8,128)(2,1)} fusion(f32[64,8192]{1,0:T(8,128)} %reshape.301, f32[64,8,8,128]{3,2,1,0:T(8,128)S(1)} %fusion.20, bf16[64,8192]{1,0:T(8,128)(2,1)S(1)} %copy-done, f32[8192]{0:T(1024)S(1)} %copy-done.8, f32[64]{0:T(128)S(1)} %copy-done.10), kind=kLoop, calls=%fused_computation.6 | loop fusion | flops 3145728 | bytes 6324480 | tf_op jit(solution)/shard_map/convert_element_type | solution.py:72
  (29 shorter events, 0.1 us)
Async XLA Ops:
  0.8 54.2 %collective-permute-start = (bf16[64,256]{1,0:T(8,128)(2,1)S(1)}, bf16[64,256]{1,0:T(8,128)(2,1)S(1)}, u32[]{:S(2)}, u32[]{:S(2)}) collective-permute-start(bf16[64,256]{1,0:T(8,128)(2,1)S(1)} %get-tuple-element.11), channel_id=1, source_target_pairs={{0,1},{1,2},{2,3},{3,4},{4,5},{5,6},{6,7},{7,8},{8,9},{9,10},{10,1... | collective-permute-start | bytes 98312 | tf_op jit(solution)/shard_map/ppermute | solution.py:19
  5.7 49.4 %collective-permute-start.1 = (bf16[64,256]{1,0:T(8,128)(2,1)S(1)}, bf16[64,256]{1,0:T(8,128)(2,1)S(1)}, u32[]{:S(2)}, u32[]{:S(2)}) collective-permute-start(bf16[64,256]{1,0:T(8,128)(2,1)S(1)} %get-tuple-element.12), channel_id=1, source_target_pairs={{1,0},{2,1},{3,2},{4,3},{5,4},{6,5},{7,6},{8,7},{9,8},{10,9},{11,1... | collective-permute-start | bytes 98312 | tf_op jit(solution)/shard_map/ppermute | solution.py:22
  30.1 8.5 %copy-start.11 = (s32[64]{0:T(128)S(1)}, s32[64]{0:T(128)}, u32[]{:S(2)}) copy-start(s32[64]{0:T(128)} %param.11) | copy-start | bytes 772
  30.1 8.5 %copy-start.9 = (s32[64,4]{0,1:T(4,128)S(1)}, s32[64,4]{0,1:T(4,128)}, u32[]{:S(2)}) copy-start(s32[64,4]{0,1:T(4,128)} %param.10) | copy-start | bytes 3076
  30.1 8.6 %copy-start = (bf16[64,8192]{1,0:T(8,128)(2,1)S(1)}, bf16[64,8192]{1,0:T(8,128)(2,1)}, u32[]{:S(2)}) copy-start(bf16[64,8192]{1,0:T(8,128)(2,1)} %param.7) | copy-start | bytes 3145732
  30.1 38.1 %all-to-all-start = ((bf16[32,2,8192]{2,1,0:T(2,128)(2,1)}), bf16[32,2,8192]{2,1,0:T(2,128)(2,1)S(1)}, u32[]{:S(2)}, u32[]{:S(2)}) async-start(bf16[32,2,8192]{2,1,0:T(2,128)(2,1)} %reshape.306), calls=%async_computation | async-start | bytes 2097152 | tf_op jit(solution)/shard_map/all_to_all | solution.py:34
  49.7 3.8 %copy-start.3 = (bf16[16,64,4,64]{3,2,1,0:T(4,128)(2,1)S(1)}, bf16[16,64,4,64]{3,2,1,0:T(4,128)(2,1)}, u32[]{:S(2)}) copy-start(bf16[16,64,4,64]{3,2,1,0:T(4,128)(2,1)} %param.8) | copy-start | bytes 1572868
  55.2 8.9 %slice-start = ((s8[8388608]{0:T(1024)(128)(4,1)}), s8[4194304]{0:T(1024)(128)(4,1)S(1)}, s32[]{:S(2)}) async-start(s8[8388608]{0:T(1024)(128)(4,1)} %bitcast.223), calls=%async_computation.4 | async-start | bytes 8388608
  55.5 4.7 %copy-start.5 = (bf16[8,64,8,128]{3,2,1,0:T(8,128)(2,1)}, bf16[8,64,8,128]{3,2,1,0:T(8,128)(2,1)S(1)}, u32[]{:S(2)}) copy-start(bf16[8,64,8,128]{3,2,1,0:T(8,128)(2,1)S(1)} %get-tuple-element.7) | copy-start | bytes 3145732
  55.6 10.6 %copy-start.1 = (bf16[8,64,8,128]{3,2,1,0:T(8,128)(2,1)}, bf16[8,64,8,128]{3,2,1,0:T(8,128)(2,1)S(1)}, u32[]{:S(2)}) copy-start(bf16[8,64,8,128]{3,2,1,0:T(8,128)(2,1)S(1)} %get-tuple-element.8) | copy-start | bytes 3145732
  55.6 8.5 %slice-start.1 = ((s8[8388608]{0:T(1024)(128)(4,1)}), s8[4194304]{0:T(1024)(128)(4,1)S(1)}, s32[]{:S(2)}) async-start(s8[8388608]{0:T(1024)(128)(4,1)} %bitcast.223), calls=%async_computation.5 | async-start | bytes 8388608
  90.0 53.6 %all-to-all-start.1 = ((bf16[16,16,64,128]{3,2,1,0:T(8,128)(2,1)}), bf16[16,16,64,128]{3,2,1,0:T(8,128)(2,1)}, u32[]{:S(2)}, u32[]{:S(2)}) async-start(bf16[16,16,64,128]{3,2,1,0:T(8,128)(2,1)} %pad_maximum_fusion), calls=%async_computation.1 | async-start | bytes 8388608 | tf_op jit(solution)/shard_map/all_to_all | solution.py:56
  95.1 1.2 copy-start.6
  95.4 16.5 %copy-start.7 = (bf16[8,64,8,128]{3,2,1,0:T(8,128)(2,1)}, bf16[8,64,8,128]{3,2,1,0:T(8,128)(2,1)S(1)}, u32[]{:S(2)}) copy-start(bf16[8,64,8,128]{3,2,1,0:T(8,128)(2,1)S(1)} %get-tuple-element.6) | copy-start | bytes 3145732
  96.3 11.4 %slice-start.2 = ((s8[8388608]{0:T(1024)(128)(4,1)}), s8[4194304]{0:T(1024)(128)(4,1)S(1)}, s32[]{:S(2)}) async-start(s8[8388608]{0:T(1024)(128)(4,1)} %bitcast.225), calls=%async_computation.6 | async-start | bytes 8388608
  100.1 3.9 %copy-start.2 = (bf16[8,64,8,128]{3,2,1,0:T(8,128)(2,1)S(1)}, bf16[8,64,8,128]{3,2,1,0:T(8,128)(2,1)}, u32[]{:S(2)}) copy-start(bf16[8,64,8,128]{3,2,1,0:T(8,128)(2,1)} %copy-done.1) | copy-start | bytes 3145732
  100.1 7.6 %slice-start.3 = ((s8[8388608]{0:T(1024)(128)(4,1)}), s8[4194304]{0:T(1024)(128)(4,1)S(1)}, s32[]{:S(2)}) async-start(s8[8388608]{0:T(1024)(128)(4,1)} %bitcast.225), calls=%async_computation.7 | async-start | bytes 8388608
  116.1 27.6 %copy-start.4 = (bf16[16,64,4,64]{1,3,0,2:T(8,128)(2,1)S(1)}, bf16[16,64,4,64]{1,3,0,2:T(8,128)(2,1)}, u32[]{:S(2)}) copy-start(bf16[16,64,4,64]{1,3,0,2:T(8,128)(2,1)} %copy.134) | copy-start | bytes 1572868
  148.1 17.6 %all-to-all-start.2 = ((bf16[16,4,64,128]{3,2,1,0:T(8,128)(2,1)}), bf16[16,4,64,128]{3,2,1,0:T(8,128)(2,1)S(1)}, u32[]{:S(2)}, u32[]{:S(2)}) async-start(bf16[16,4,64,128]{3,2,1,0:T(8,128)(2,1)} %fusion.48), calls=%async_computation.2 | async-start | bytes 2097152 | tf_op jit(solution)/shard_map/all_to_all | solution.py:61
  167.4 25.9 %all-to-all-start.3 = ((bf16[4,16,64,128]{3,1,0,2:T(8,128)(2,1)}), bf16[4,16,64,128]{3,1,0,2:T(8,128)(2,1)}, u32[]{:S(2)}, u32[]{:S(2)}) async-start(bf16[4,16,64,128]{3,1,0,2:T(8,128)(2,1)} %copy.136), calls=%async_computation.3 | async-start | bytes 2097152 | tf_op jit(solution)/shard_map/all_to_all | solution.py:60
  197.6 2.8 %copy-start.8 = (f32[8192]{0:T(1024)S(1)}, f32[8192]{0:T(1024)}, u32[]{:S(2)}) copy-start(f32[8192]{0:T(1024)} %param.13) | copy-start | bytes 98308
  197.6 2.8 %copy-start.10 = (f32[64]{0:T(128)S(1)}, f32[64]{0:T(128)}, u32[]{:S(2)}) copy-start(f32[64]{0:T(128)} %param.12) | copy-start | bytes 772
